TPU v7x, 32 devices: a whole 2x2x4 slice. The times are simulated.
32 devices in a mesh: seq: 16 (over z, y, x), batch: 2 (over core).
Axes of the slice: x: 2, y: 2, z: 4, core: 2. Of those that a mesh axis runs over, the one named last changes fastest.
Arguments:
- inputs: bfloat16 [16, 2048, 1024], P('batch', 'seq'), may hold values from -6 to 6
- segments: int32 [16, 2048], P('batch', 'seq'), may hold values from 0 to 2, as said below
- groups: int32 [16, 2048], P('batch', 'seq'), may hold values from 0 to 7
- group_loss_weight: float32 [8], replicated, may hold values from 0.5 to 2
- attention_norm_gain: bfloat16 [1024], replicated, may hold values from 0.5 to 1.5
- attention_norm_bias: bfloat16 [1024], replicated, may hold values from -1.75 to 1.75
- query_key_value_weight: bfloat16 [1024, 3072], replicated, may hold values from -0.1875 to 0.1875
- query_value_bias: bfloat16 [2, 1024], replicated, may hold values from -1.75 to 1.75
- attention_out_weight: bfloat16 [1024, 1024], replicated, may hold values from -0.75 to 0.75
- attention_out_bias: bfloat16 [1024], replicated, may hold values from -1.75 to 1.75
- feedforward_norm_gain: bfloat16 [1024], replicated, may hold values from 0.099609375 to 1.8984375
- feedforward_norm_bias: bfloat16 [1024], replicated, may hold values from -1.75 to 1.75
- expand_weight: bfloat16 [1024, 4096], replicated, may hold values from -0.1875 to 0.1875
- expand_bias: bfloat16 [4096], replicated, may hold values from -1.75 to 1.75
- contract_weight: bfloat16 [4096, 1024], replicated, may hold values from -0.09375 to 0.09375
- contract_bias: bfloat16 [1024], replicated, may hold values from -1.75 to 1.75
- adapter_down_maps: float32 [2, 1024, 4], replicated, may hold values from -0.1875 to 0.1875
- adapter_up_maps: float32 [2, 4, 1024], replicated, may hold values from -0.375 to 0.375
- down_velocity: float32 [2, 1024, 4], replicated, may hold values from -6144 to 6144
- up_velocity: float32 [2, 4, 1024], replicated, may hold values from -3072 to 3072
- running_down_mean: float32 [2, 1024, 4], replicated, may hold values from -0.1875 to 0.1875
- running_up_mean: float32 [2, 4, 1024], replicated, may hold values from -0.375 to 0.375
- cotangent: bfloat16 [16, 2048, 1024], P('batch', 'seq'), may hold values from -6 to 6
Outputs:
- layer_output: bfloat16 [16, 2048, 1024], P('batch', 'seq')
- input_grad: bfloat16 [16, 2048, 1024], P('batch', 'seq')
- lora_a_grad: float32 [2, 1024, 4], replicated
- lora_b_grad: float32 [2, 4, 1024], replicated
- adapter_down_updated: float32 [2, 1024, 4], replicated
- adapter_up_updated: float32 [2, 4, 1024], replicated
- down_velocity_next: float32 [2, 1024, 4], replicated
- up_velocity_next: float32 [2, 4, 1024], replicated
- updated_down_mean: float32 [2, 1024, 4], replicated
- updated_up_mean: float32 [2, 4, 1024], replicated
- lora_a_copy: bfloat16 [2, 1024, 4], replicated
- lora_b_copy: bfloat16 [2, 4, 1024], replicated
Inputs may be any that keep to these rules, and one draw needn't show every extreme that they name: `segments`: in each row the segment numbers start at 0, never fall and rise by one from one example to the next; every example has 1 to 1024 tokens, the second example of each row has exactly 1024 tokens, and every row holds the same number of examples.
All inputs are finite; a program needn't handle non-finite values.
Results may differ from a plain program's by a relative error of at most 0.019.
Values may be sent and summed in bfloat16 or wider, within the bound.
No kernel may reach another device: no remote copies, remote signals or barrier semaphores. Data moves between devices by JAX's collectives and lax.ppermute only.
A program may use at most 576 MiB of HBM per device.

v0:
```python
import math

import jax
import jax.numpy as jnp
from jax import lax
from jax.sharding import PartitionSpec as P

HEADS = 16
EXAMPLE_MAX = 1024


norm_eps = 1e-05
adapter_scale = 8.0
learning_step_size = 3e-05
velocity_factor = 0.5
mean_decay_factor = 0.5
masked_score = -1e30
score_scale = 0.125


def passed_along(x, axis, by):
    devices = lax.axis_size(axis)
    pairs = [(i, i + by) for i in range(devices) if 0 <= i + by < devices]
    return lax.ppermute(x, axis, pairs)


def norm_layer(values, gain_row, shift_row):
    average = jnp.mean(values, axis=-1, keepdims=True)
    centred = values - average
    variance = jnp.mean(centred * centred, axis=-1, keepdims=True)
    return centred * lax.rsqrt(variance + norm_eps) * gain_row + shift_row


def matmul_rows(left_side, right_side):
    return lax.dot_general(
        left_side,
        right_side,
        (((left_side.ndim - 1,), (0,)), ((), ())),
        preferred_element_type=jnp.float32,
    )


def matmul_back(left_side, right_side):
    return lax.dot_general(
        left_side,
        right_side,
        (((left_side.ndim - 1,), (1,)), ((), ())),
        preferred_element_type=jnp.float32,
    )


def split_heads(one_block):
    return one_block.reshape(one_block.shape[:-1] + (HEADS, one_block.shape[-1] // HEADS))


def gelu_tanh(values):
    return jax.nn.gelu(values, approximate=True)


def block_scores(query_heads, query_seg, query_place, row_total, key_block, seg_block, block_start):
    half_width = key_block.shape[-1] // 2
    key_heads = split_heads(key_block[..., :half_width])
    value_heads = split_heads(key_block[..., half_width:])
    scores = (
        jnp.einsum("rqhe,rkhe->rhqk", query_heads, key_heads, preferred_element_type=jnp.float32)
        * score_scale
    )
    key_place = block_start + jnp.arange(key_block.shape[1], dtype=jnp.int32)
    order_ok = (key_place[None, :] <= query_place[:, None]) & (key_place[None, :] >= 0)
    order_ok = order_ok & (query_place[:, None] < row_total)
    allowed = (seg_block[:, None, :] == query_seg[:, :, None]) & order_ok[None, :, :]
    allowed = allowed[:, None, :, :]
    return (jnp.where(allowed, scores, masked_score), allowed, key_heads, value_heads)


def over_blocks(block_step, carry_start, key_all, seg_all, key_start):
    length = key_all.shape[1]
    block_width = math.gcd(length, 512)

    def visit_block(carry_state, block_index):
        offset = block_index * block_width
        key_block = lax.dynamic_slice_in_dim(key_all, offset, block_width, 1)
        seg_block = lax.dynamic_slice_in_dim(seg_all, offset, block_width, 1)
        return (block_step(carry_state, key_block, seg_block, key_start + offset), None)

    carry_end, _ = lax.scan(
        visit_block, carry_start, jnp.arange(length // block_width, dtype=jnp.int32)
    )
    return carry_end


def body(
    inputs,
    segments,
    groups,
    group_loss_weight,
    attention_norm_gain,
    attention_norm_bias,
    query_key_value_weight,
    query_value_bias,
    attention_out_weight,
    attention_out_bias,
    feedforward_norm_gain,
    feedforward_norm_bias,
    expand_weight,
    expand_bias,
    contract_weight,
    contract_bias,
    adapter_down_maps,
    adapter_up_maps,
    down_velocity,
    up_velocity,
    running_down_mean,
    running_up_mean,
    cotangent,
):
    batch_rows = inputs.shape[0]
    local_count = inputs.shape[1]
    hidden_width = inputs.shape[2]
    head_width = hidden_width // HEADS
    reach = (EXAMPLE_MAX - 1) // local_count + 1
    values_in = inputs.astype(jnp.float32)

    def first_norm(values):
        return norm_layer(
            values, attention_norm_gain.astype(jnp.float32), attention_norm_bias.astype(jnp.float32)
        )

    def second_norm(values):
        return norm_layer(
            values,
            feedforward_norm_gain.astype(jnp.float32),
            feedforward_norm_bias.astype(jnp.float32),
        )

    normed_low = first_norm(values_in).astype(jnp.bfloat16)
    projected_rows = matmul_rows(normed_low, query_key_value_weight)
    down_reduced = adapter_down_maps.astype(jnp.bfloat16)
    up_reduced = adapter_up_maps.astype(jnp.bfloat16)
    adapter_down_apply = jnp.einsum(
        "rnd,jdk->jrnk", normed_low, down_reduced, preferred_element_type=jnp.float32
    ).astype(jnp.bfloat16)
    adapter_up_apply = jnp.einsum(
        "gslt,gtf->gslf", adapter_down_apply, up_reduced, preferred_element_type=jnp.float32
    )
    bias_as_float = query_value_bias.astype(jnp.float32)
    query_matrix = (
        projected_rows[..., :hidden_width] + bias_as_float[0] + adapter_scale * adapter_up_apply[0]
    ).astype(jnp.bfloat16)
    key_rows = projected_rows[..., hidden_width : 2 * hidden_width].astype(jnp.bfloat16)
    value_matrix = (
        projected_rows[..., 2 * hidden_width :]
        + bias_as_float[1]
        + adapter_scale * adapter_up_apply[1]
    ).astype(jnp.bfloat16)
    key_value = jnp.concatenate([key_rows, value_matrix], axis=-1)
    seg_low = segments.astype(jnp.bfloat16)
    query_heads = split_heads(query_matrix)
    my_start = lax.axis_index("seq") * local_count
    row_total = lax.axis_size("seq") * local_count
    query_place = my_start + jnp.arange(local_count, dtype=jnp.int32)
    key_list = []
    seg_list = []
    for step in range(reach, 0, -1):
        near_keys, near_seg = passed_along((key_value, seg_low), "seq", step)
        key_list.append(near_keys)
        seg_list.append(near_seg)
    key_all = jnp.concatenate(key_list + [key_value], axis=1)
    seg_all = jnp.concatenate(seg_list + [seg_low], axis=1)
    key_start = my_start - reach * local_count

    def forward_step(carry_state, key_block, seg_block, block_start):
        weighted_sum, running, denominator = carry_state
        scores, allowed, _, value_heads = block_scores(
            query_heads, seg_low, query_place, row_total, key_block, seg_block, block_start
        )
        newtop = jnp.maximum(running, jnp.max(scores, axis=-1))
        weights = jnp.where(allowed, jnp.exp(scores - newtop[..., None]), 0.0)
        rescale = jnp.exp(running - newtop)
        denominator = denominator * rescale + jnp.sum(weights, axis=-1)
        contribution = jnp.einsum(
            "rhqk,rkhe->rqhe",
            weights.astype(jnp.bfloat16),
            value_heads,
            preferred_element_type=jnp.float32,
        )
        weighted_sum = weighted_sum * jnp.transpose(rescale, (0, 2, 1))[..., None] + contribution
        return (weighted_sum, newtop, denominator)

    start_state = (
        jnp.zeros((batch_rows, local_count, HEADS, head_width), jnp.float32),
        jnp.full((batch_rows, HEADS, local_count), masked_score, jnp.float32),
        jnp.zeros((batch_rows, HEADS, local_count), jnp.float32),
    )
    weighted_sum, running, denominator = over_blocks(
        forward_step, start_state, key_all, seg_all, key_start
    )
    attend = weighted_sum * jnp.transpose(1.0 / denominator, (0, 2, 1))[..., None]
    log_total = running + jnp.log(denominator)
    attend_low = attend.reshape(batch_rows, local_count, hidden_width).astype(jnp.bfloat16)
    middle = (
        values_in
        + matmul_rows(attend_low, attention_out_weight)
        + attention_out_bias.astype(jnp.float32)
    )
    normed_two_low = second_norm(middle).astype(jnp.bfloat16)
    pre_act = matmul_rows(normed_two_low, expand_weight) + expand_bias.astype(jnp.float32)
    act_low = gelu_tanh(pre_act).astype(jnp.bfloat16)
    layer_result = (
        middle + matmul_rows(act_low, contract_weight) + contract_bias.astype(jnp.float32)
    )
    chooser = (groups[..., None] == jnp.arange(group_loss_weight.shape[0], dtype=jnp.int32)).astype(
        jnp.float32
    )
    token_weight = jnp.einsum("rng,g->rn", chooser, group_loss_weight)
    grad_out = cotangent.astype(jnp.float32) * token_weight[..., None]
    grad_act = matmul_back(grad_out.astype(jnp.bfloat16), contract_weight)
    _, gelu_pull = jax.vjp(gelu_tanh, pre_act)
    grad_pre = gelu_pull(grad_act)[0].astype(jnp.bfloat16)
    _, second_pull = jax.vjp(second_norm, middle)
    grad_middle = grad_out + second_pull(matmul_back(grad_pre, expand_weight))[0]
    grad_attend = matmul_back(grad_middle.astype(jnp.bfloat16), attention_out_weight).astype(
        jnp.bfloat16
    )
    grad_heads = split_heads(grad_attend)
    grad_dot = jnp.transpose(jnp.sum(grad_heads.astype(jnp.float32) * attend, axis=-1), (0, 2, 1))
    local_side = (query_heads, grad_heads, seg_low, query_place, log_total, grad_dot)

    def pair_grads(query_side, key_block, seg_block, block_start):
        side_heads, side_grads, side_seg, side_place, side_log, side_dot = query_side
        scores, allowed, key_heads, value_heads = block_scores(
            side_heads, side_seg, side_place, row_total, key_block, seg_block, block_start
        )
        weights_norm = jnp.where(allowed, jnp.exp(scores - side_log[..., None]), 0.0)
        grad_weights = jnp.einsum(
            "rqhe,rkhe->rhqk", side_grads, value_heads, preferred_element_type=jnp.float32
        )
        grad_scores = (weights_norm * (grad_weights - side_dot[..., None])).astype(jnp.bfloat16)
        return (weights_norm, grad_scores, key_heads)

    def query_step(carry_state, key_block, seg_block, block_start):
        _, grad_scores, key_heads = pair_grads(local_side, key_block, seg_block, block_start)
        return carry_state + score_scale * jnp.einsum(
            "rhqk,rkhe->rqhe", grad_scores, key_heads, preferred_element_type=jnp.float32
        )

    grad_queries = over_blocks(
        query_step,
        jnp.zeros((batch_rows, local_count, HEADS, head_width), jnp.float32),
        key_all,
        seg_all,
        key_start,
    )
    query_reduced_gradient = grad_queries.reshape(batch_rows, local_count, hidden_width).astype(
        jnp.bfloat16
    )

    def key_step(query_side, key_block, seg_block, block_start):
        weights_norm, grad_scores, _ = pair_grads(query_side, key_block, seg_block, block_start)
        grad_keys = score_scale * jnp.einsum(
            "rhqk,rqhe->rkhe", grad_scores, query_side[0], preferred_element_type=jnp.float32
        )
        grad_values = jnp.einsum(
            "rhqk,rqhe->rkhe",
            weights_norm.astype(jnp.bfloat16),
            query_side[1],
            preferred_element_type=jnp.float32,
        )
        return (grad_keys, grad_values)

    total_rows = key_all.shape[1]
    block_width = math.gcd(total_rows, 512)

    def visit_keys(block_index):
        offset = block_index * block_width
        key_block = lax.dynamic_slice_in_dim(key_all, offset, block_width, 1)
        seg_block = lax.dynamic_slice_in_dim(seg_all, offset, block_width, 1)
        grad_keys, grad_values = key_step(local_side, key_block, seg_block, key_start + offset)
        joined = jnp.concatenate(
            [
                grad_keys.reshape(batch_rows, block_width, hidden_width),
                grad_values.reshape(batch_rows, block_width, hidden_width),
            ],
            axis=-1,
        )
        return jnp.transpose(joined, (1, 0, 2))

    terms = lax.map(visit_keys, jnp.arange(total_rows // block_width, dtype=jnp.int32))
    terms = terms.reshape(total_rows, batch_rows, 2 * hidden_width)
    own_sum = terms[reach * local_count :]
    for step in range(1, reach + 1):
        piece = lax.slice_in_dim(
            terms, (reach - step) * local_count, (reach - step + 1) * local_count, axis=0
        )
        own_sum = own_sum + passed_along(piece.astype(jnp.bfloat16), "seq", -step).astype(
            piece.dtype
        )
    key_sums = jnp.transpose(own_sum, (1, 0, 2)).astype(jnp.bfloat16)
    grad_k_low = key_sums[..., :hidden_width]
    value_reduced_gradient = key_sums[..., hidden_width:]
    adapter_output_gradient = jnp.stack([query_reduced_gradient, value_reduced_gradient])
    up_map_gradient = adapter_scale * jnp.einsum(
        "sbfp,sbfh->sph",
        adapter_down_apply,
        adapter_output_gradient,
        preferred_element_type=jnp.float32,
    )
    grad_down = (
        adapter_scale
        * jnp.einsum(
            "zbtu,zxu->zbtx",
            adapter_output_gradient,
            up_reduced,
            preferred_element_type=jnp.float32,
        )
    ).astype(jnp.bfloat16)
    down_map_gradient = jnp.einsum(
        "rnd,jrnk->jdk", normed_low, grad_down, preferred_element_type=jnp.float32
    )
    grad_normed = matmul_back(
        jnp.concatenate([query_reduced_gradient, grad_k_low, value_reduced_gradient], axis=-1),
        query_key_value_weight,
    )
    grad_normed = grad_normed + jnp.einsum(
        "jrnk,jdk->rnd", grad_down, down_reduced, preferred_element_type=jnp.float32
    )
    _, first_pull = jax.vjp(first_norm, values_in)
    gradient_incoming = (grad_middle + first_pull(grad_normed)[0]).astype(jnp.bfloat16)
    down_map_gradient, up_map_gradient = lax.psum(
        (down_map_gradient, up_map_gradient), ("seq", "batch")
    )
    down_velocity_next = velocity_factor * down_velocity + down_map_gradient
    up_velocity_next = velocity_factor * up_velocity + up_map_gradient
    adapter_down_updated = adapter_down_maps - learning_step_size * (
        down_map_gradient + velocity_factor * down_velocity_next
    )
    adapter_up_updated = adapter_up_maps - learning_step_size * (
        up_map_gradient + velocity_factor * up_velocity_next
    )
    updated_down_mean = (
        mean_decay_factor * running_down_mean + (1.0 - mean_decay_factor) * adapter_down_updated
    )
    updated_up_mean = (
        mean_decay_factor * running_up_mean + (1.0 - mean_decay_factor) * adapter_up_updated
    )
    return (
        layer_result.astype(jnp.bfloat16),
        gradient_incoming,
        down_map_gradient,
        up_map_gradient,
        adapter_down_updated,
        adapter_up_updated,
        down_velocity_next,
        up_velocity_next,
        updated_down_mean,
        updated_up_mean,
        adapter_down_updated.astype(jnp.bfloat16),
        adapter_up_updated.astype(jnp.bfloat16),
    )


def solution(mesh):
    placed = (
        P("batch", "seq", None),
        P("batch", "seq"),
        P("batch", "seq"),
        P(),
        P(),
        P(),
        P(),
        P(),
        P(),
        P(),
        P(),
        P(),
        P(),
        P(),
        P(),
        P(),
        P(),
        P(),
        P(),
        P(),
        P(),
        P(),
        P("batch", "seq", None),
    )
    return jax.shard_map(
        body,
        mesh=mesh,
        in_specs=placed,
        out_specs=(
            P("batch", "seq", None),
            P("batch", "seq", None),
            P(),
            P(),
            P(),
            P(),
            P(),
            P(),
            P(),
            P(),
            P(),
            P(),
        ),
        check_vma=False,
    )
```

profile of v0, /device:TPU:0, one launch (start us, length us, event | category | flops | bytes accessed | tf_op | source)
XLA Modules:
  0.0 3174.6 jit_solution(1731632425432124372)
XLA Ops:
  54.9 342.5 %collective-permute-done = bf16[8,128]{1,0:T(8,128)(2,1)S(1)} collective-permute-done((bf16[8,128]{1,0:T(8,128)(2,1)S(1)}, bf16[8,128]{1,0:T(8,128)(2,1)S(1)}, u32[]{:S(2)}, u32[]{:S(2)}) %collective-permute-start) | collective-permute-done | bytes 2080 | tf_op jit(solution)/shard_map/ppermute | solution.py:24
  397.4 364.9 %collective-permute-start.1 = (bf16[8,128]{1,0:T(8,128)(2,1)S(1)}, bf16[8,128]{1,0:T(8,128)(2,1)S(1)}, u32[]{:S(2)}, u32[]{:S(2)}) collective-permute-start(bf16[8,128]{1,0:T(8,128)(2,1)S(1)} %convert_element_type.191), channel_id=1, source_target_pairs={{0,14},{2,16},{4,18},{6,20},{8,22},{10,24},{12,26},{14,28},{16,30}... | collective-permute-start | bytes 6152 | tf_op jit(solution)/shard_map/ppermute | solution.py:24
  797.5 12.7 collective-permute-start.12
  848.3 42.3 %collective-permute-done.12 = bf16[8,128,2048]{2,1,0:T(8,128)(2,1)} collective-permute-done((bf16[8,128,2048]{2,1,0:T(8,128)(2,1)}, bf16[8,128,2048]{2,1,0:T(8,128)(2,1)}, u32[]{:S(2)}, u32[]{:S(2)}) %collective-permute-start.12) | collective-permute-done | bytes 4194336 | tf_op jit(solution)/shard_map/ppermute | solution.py:24
  908.7 79.2 %collective-permute-done.14 = bf16[8,128,2048]{2,1,0:T(8,128)(2,1)} collective-permute-done((bf16[8,128,2048]{2,1,0:T(8,128)(2,1)}, bf16[8,128,2048]{2,1,0:T(8,128)(2,1)}, u32[]{:S(2)}, u32[]{:S(2)}) %collective-permute-start.14) | collective-permute-done | bytes 4194336 | tf_op jit(solution)/shard_map/ppermute | solution.py:24
  1000.1 44.1 %copy.58 = bf16[8,1152,2048]{1,2,0:T(8,128)(2,1)} copy(bf16[8,1152,2048]{2,1,0:T(8,128)(2,1)} %constant_dynamic-update-slice_fusion.10) | data formatting | bytes 75497472
  1044.2 110.5 %while.38 = (s32[]{:T(128)}, f32[8,128,16,64]{1,3,2,0:T(8,128)}, f32[8,16,128]{2,1,0:T(8,128)S(1)}, f32[8,16,128]{2,1,0:T(8,128)S(1)}, s32[9]{0:T(128)S(1)}, /*i...) while((s32[]{:T(128)}, f32[8,128,16,64]{1,3,2,0:T(8,128)}, ...), condition=%wide.region_5.6_spmd.clone, body=%wide.region_2.5_spmd.clone.sunk | while | flops 567952128 | bytes 91794272 | solution.py:86
  1161.3 12.2 fusion.91
  1173.5 31.0 multiply_reduce_fusion.1
  1223.0 478.0 %while.37 = (s32[]{:T(128)}, f32[9,128,8,2048]{3,1,2,0:T(8,128)}, s32[9]{0:T(128)S(1)}, bf16[8,1152]{1,0:T(8,128)(2,1)S(1)}, bf16[8,128]{1,0:T(8,128)(2,1)S(1)},...) while((s32[]{:T(128)}, f32[9,128,8,2048]{3,1,2,0:T(8,128)}, ...), condition=%wide.region_14.15_spmd.clone, body=%wide.region_13.14_spmd.clone.sunk | while | flops 1102627584 | bytes 105491216 | solution.py:288
  1701.0 36.3 %convert.14 = bf16[9,128,8,2048]{3,1,2,0:T(8,128)(2,1)} convert(f32[9,128,8,2048]{3,1,2,0:T(8,128)} %get-tuple-element.199) | non-fusion elementwise | flops 18874368 | bytes 113246208 | tf_op jit(solution)/shard_map/convert.7
  1737.3 23.3 slice_bitcast_fusion.7
  1777.1 599.5 %collective-permute-done.23 = bf16[128,8,2048]{2,0,1:T(8,128)(2,1)} collective-permute-done((bf16[128,8,2048]{2,0,1:T(8,128)(2,1)}, bf16[128,8,2048]{2,0,1:T(8,128)(2,1)}, u32[]{:S(2)}, u32[]{:S(2)}) %collective-permute-start.23) | collective-permute-done | bytes 4194336 | tf_op jit(solution)/shard_map/ppermute | solution.py:24
  2380.5 195.8 %while.39 = (s32[]{:T(128)}, f32[8,128,16,64]{1,3,2,0:T(8,128)}, s32[9]{0:T(128)S(1)}, bf16[8,1152,2048]{1,2,0:T(8,128)(2,1)}, bf16[8,1152]{1,0:T(8,128)(2,1)S(1...) while((s32[]{:T(128)}, f32[8,128,16,64]{1,3,2,0:T(8,128)}, ...), condition=%wide.region_12.13_spmd.clone, body=%wide.region_11.12_spmd.clone.sunk | while | flops 823706368 | bytes 50768696 | solution.py:86
  2411.8 11.6 bitcast_add_fusion.7
  2433.7 11.6 bitcast_add_fusion.7
  2455.5 11.6 bitcast_add_fusion.7
  2477.4 11.6 bitcast_add_fusion.7
  2499.2 11.6 bitcast_add_fusion.7
  2521.0 11.6 bitcast_add_fusion.7
  2584.2 18.3 add_convert_fusion.1
  2602.6 17.3 fusion.121
  2629.9 11.6 fusion.109
  2650.4 510.2 %all-reduce.3.cloned.1.call-done = (f32[2,1024,4]{1,2,0:T(4,128)}, f32[2,4,1024]{2,1,0:T(4,128)}) async-done(((f32[2,1024,4]{1,2,0:T(4,128)}, f32[2,4,1024]{2,1,0:T(4,128)}), (f32[2,1024,4]{1,2,0:T(4,128)}, f32[2,4,1024]{2,1,0:T(4,128)})) %all-reduce.3.cloned.1.call-update) | async-done | bytes 65552 | tf_op jit(solution)/shard_map/psum | solution.py:329
  (615 shorter events, 924.8 us)
Async XLA Ops:
  7.2 3153.5 %all-reduce.3.cloned.1.call-start = ((), (), s32[]{:S(2)}) async-start(), calls=%async_computation | async-start | bytes 131072 | tf_op jit(solution)/shard_map/psum | solution.py:329
  31.5 778.6 %collective-permute-start.8 = (bf16[8,128,2048]{2,1,0:T(8,128)(2,1)}, bf16[8,128,2048]{2,1,0:T(8,128)(2,1)}, u32[]{:S(2)}, u32[]{:S(2)}) collective-permute-start(bf16[8,128,2048]{2,1,0:T(8,128)(2,1)} %pad_maximum_fusion), channel_id=1, source_target_pairs={{0,16},{2,18},{4,20},{6,22},{8,24},{10,26},{12,28},{14,30},{1,17},... | collective-permute-start | bytes 12582920 | tf_op jit(solution)/shard_map/ppermute | solution.py:24
  39.6 774.9 %collective-permute-start.9 = (bf16[8,128,2048]{2,1,0:T(8,128)(2,1)}, bf16[8,128,2048]{2,1,0:T(8,128)(2,1)}, u32[]{:S(2)}, u32[]{:S(2)}) collective-permute-start(bf16[8,128,2048]{2,1,0:T(8,128)(2,1)} %pad_maximum_fusion), channel_id=1, source_target_pairs={{0,14},{2,16},{4,18},{6,20},{8,22},{10,24},{12,26},{14,28},{16,30}... | collective-permute-start | bytes 12582920 | tf_op jit(solution)/shard_map/ppermute | solution.py:24
  46.9 770.9 %collective-permute-start.10 = (bf16[8,128,2048]{2,1,0:T(8,128)(2,1)}, bf16[8,128,2048]{2,1,0:T(8,128)(2,1)}, u32[]{:S(2)}, u32[]{:S(2)}) collective-permute-start(bf16[8,128,2048]{2,1,0:T(8,128)(2,1)} %pad_maximum_fusion), channel_id=1, source_target_pairs={{0,12},{2,14},{4,16},{6,18},{8,20},{10,22},{12,24},{14,26},{16,28}... | collective-permute-start | bytes 12582920 | tf_op jit(solution)/shard_map/ppermute | solution.py:24
  50.4 793.1 %collective-permute-start.11 = (bf16[8,128,2048]{2,1,0:T(8,128)(2,1)}, bf16[8,128,2048]{2,1,0:T(8,128)(2,1)}, u32[]{:S(2)}, u32[]{:S(2)}) collective-permute-start(bf16[8,128,2048]{2,1,0:T(8,128)(2,1)} %pad_maximum_fusion), channel_id=1, source_target_pairs={{0,10},{2,12},{4,14},{6,16},{8,18},{10,20},{12,22},{14,24},{16,26}... | collective-permute-start | bytes 12582920 | tf_op jit(solution)/shard_map/ppermute | solution.py:24
  53.6 343.8 %collective-permute-start = (bf16[8,128]{1,0:T(8,128)(2,1)S(1)}, bf16[8,128]{1,0:T(8,128)(2,1)S(1)}, u32[]{:S(2)}, u32[]{:S(2)}) collective-permute-start(bf16[8,128]{1,0:T(8,128)(2,1)S(1)} %convert_element_type.191), channel_id=1, source_target_pairs={{0,16},{2,18},{4,20},{6,22},{8,24},{10,26},{12,28},{14,30},{1,17},... | collective-permute-start | bytes 6152 | tf_op jit(solution)/shard_map/ppermute | solution.py:24
  397.4 366.2 %collective-permute-start.1 = (bf16[8,128]{1,0:T(8,128)(2,1)S(1)}, bf16[8,128]{1,0:T(8,128)(2,1)S(1)}, u32[]{:S(2)}, u32[]{:S(2)}) collective-permute-start(bf16[8,128]{1,0:T(8,128)(2,1)S(1)} %convert_element_type.191), channel_id=1, source_target_pairs={{0,14},{2,16},{4,18},{6,20},{8,22},{10,24},{12,26},{14,28},{16,30}... | collective-permute-start | bytes 6152 | tf_op jit(solution)/shard_map/ppermute | solution.py:24
  763.6 2.6 collective-permute-start.2
  768.8 12.4 collective-permute-start.4
  781.1 6.2 collective-permute-start.5
  787.4 4.8 collective-permute-start.6
  792.1 5.3 collective-permute-start.7
  797.5 93.1 %collective-permute-start.12 = (bf16[8,128,2048]{2,1,0:T(8,128)(2,1)}, bf16[8,128,2048]{2,1,0:T(8,128)(2,1)}, u32[]{:S(2)}, u32[]{:S(2)}) collective-permute-start(bf16[8,128,2048]{2,1,0:T(8,128)(2,1)} %pad_maximum_fusion), channel_id=1, source_target_pairs={{0,8},{2,10},{4,12},{6,14},{8,16},{10,18},{12,20},{14,22},{16,24},... | collective-permute-start | bytes 12582920 | tf_op jit(solution)/shard_map/ppermute | solution.py:24
  810.2 93.7 %collective-permute-start.13 = (bf16[8,128,2048]{2,1,0:T(8,128)(2,1)}, bf16[8,128,2048]{2,1,0:T(8,128)(2,1)}, u32[]{:S(2)}, u32[]{:S(2)}) collective-permute-start(bf16[8,128,2048]{2,1,0:T(8,128)(2,1)} %pad_maximum_fusion), channel_id=1, source_target_pairs={{0,6},{2,8},{4,10},{6,12},{8,14},{10,16},{12,18},{14,20},{16,22},{... | collective-permute-start | bytes 12582920 | tf_op jit(solution)/shard_map/ppermute | solution.py:24
  814.5 173.5 %collective-permute-start.14 = (bf16[8,128,2048]{2,1,0:T(8,128)(2,1)}, bf16[8,128,2048]{2,1,0:T(8,128)(2,1)}, u32[]{:S(2)}, u32[]{:S(2)}) collective-permute-start(bf16[8,128,2048]{2,1,0:T(8,128)(2,1)} %pad_maximum_fusion), channel_id=1, source_target_pairs={{0,4},{2,6},{4,8},{6,10},{8,12},{10,14},{12,16},{14,18},{16,20},{1... | collective-permute-start | bytes 12582920 | tf_op jit(solution)/shard_map/ppermute | solution.py:24
  817.9 174.9 %collective-permute-start.15 = (bf16[8,128,2048]{2,1,0:T(8,128)(2,1)}, bf16[8,128,2048]{2,1,0:T(8,128)(2,1)}, u32[]{:S(2)}, u32[]{:S(2)}) collective-permute-start(bf16[8,128,2048]{2,1,0:T(8,128)(2,1)} %pad_maximum_fusion), channel_id=1, source_target_pairs={{0,2},{2,4},{4,6},{6,8},{8,10},{10,12},{12,14},{14,16},{16,18},{18... | collective-permute-start | bytes 12582920 | tf_op jit(solution)/shard_map/ppermute | solution.py:24
  1760.6 616.0 %collective-permute-start.23 = (bf16[128,8,2048]{2,0,1:T(8,128)(2,1)}, bf16[128,8,2048]{2,0,1:T(8,128)(2,1)}, u32[]{:S(2)}, u32[]{:S(2)}) collective-permute-start(bf16[128,8,2048]{2,0,1:T(8,128)(2,1)} %get-tuple-element.481), channel_id=1, source_target_pairs={{16,0},{18,2},{20,4},{22,6},{24,8},{26,10},{28,12},{30,14},{17,1},... | collective-permute-start | bytes 12582920 | tf_op jit(solution)/shard_map/ppermute | solution.py:24
  1761.9 616.0 %collective-permute-start.22 = (bf16[128,8,2048]{2,0,1:T(8,128)(2,1)}, bf16[128,8,2048]{2,0,1:T(8,128)(2,1)}, u32[]{:S(2)}, u32[]{:S(2)}) collective-permute-start(bf16[128,8,2048]{2,0,1:T(8,128)(2,1)} %get-tuple-element.482), channel_id=1, source_target_pairs={{14,0},{16,2},{18,4},{20,6},{22,8},{24,10},{26,12},{28,14},{30,16}... | collective-permute-start | bytes 12582920 | tf_op jit(solution)/shard_map/ppermute | solution.py:24
  1763.2 616.0 %collective-permute-start.21 = (bf16[128,8,2048]{2,0,1:T(8,128)(2,1)}, bf16[128,8,2048]{2,0,1:T(8,128)(2,1)}, u32[]{:S(2)}, u32[]{:S(2)}) collective-permute-start(bf16[128,8,2048]{2,0,1:T(8,128)(2,1)} %get-tuple-element.483), channel_id=1, source_target_pairs={{12,0},{14,2},{16,4},{18,6},{20,8},{22,10},{24,12},{26,14},{28,16}... | collective-permute-start | bytes 12582920 | tf_op jit(solution)/shard_map/ppermute | solution.py:24
  1774.5 828.0 %collective-permute-start.20 = (bf16[128,8,2048]{2,0,1:T(8,128)(2,1)}, bf16[128,8,2048]{2,0,1:T(8,128)(2,1)}, u32[]{:S(2)}, u32[]{:S(2)}) collective-permute-start(bf16[128,8,2048]{2,0,1:T(8,128)(2,1)} %get-tuple-element.484), channel_id=1, source_target_pairs={{10,0},{12,2},{14,4},{16,6},{18,8},{20,10},{22,12},{24,14},{26,16}... | collective-permute-start | bytes 12582920 | tf_op jit(solution)/shard_map/ppermute | solution.py:24
  1775.8 826.8 %collective-permute-start.19 = (bf16[128,8,2048]{2,0,1:T(8,128)(2,1)}, bf16[128,8,2048]{2,0,1:T(8,128)(2,1)}, u32[]{:S(2)}, u32[]{:S(2)}) collective-permute-start(bf16[128,8,2048]{2,0,1:T(8,128)(2,1)} %get-tuple-element.485), channel_id=1, source_target_pairs={{8,0},{10,2},{12,4},{14,6},{16,8},{18,10},{20,12},{22,14},{24,16},... | collective-permute-start | bytes 12582920 | tf_op jit(solution)/shard_map/ppermute | solution.py:24
  2376.6 226.0 %collective-permute-start.18 = (bf16[128,8,2048]{2,0,1:T(8,128)(2,1)}, bf16[128,8,2048]{2,0,1:T(8,128)(2,1)}, u32[]{:S(2)}, u32[]{:S(2)}) collective-permute-start(bf16[128,8,2048]{2,0,1:T(8,128)(2,1)} %get-tuple-element.486), channel_id=1, source_target_pairs={{6,0},{8,2},{10,4},{12,6},{14,8},{16,10},{18,12},{20,14},{22,16},{... | collective-permute-start | bytes 12582920 | tf_op jit(solution)/shard_map/ppermute | solution.py:24
  2377.9 224.7 %collective-permute-start.17 = (bf16[128,8,2048]{2,0,1:T(8,128)(2,1)}, bf16[128,8,2048]{2,0,1:T(8,128)(2,1)}, u32[]{:S(2)}, u32[]{:S(2)}) collective-permute-start(bf16[128,8,2048]{2,0,1:T(8,128)(2,1)} %get-tuple-element.487), channel_id=1, source_target_pairs={{4,0},{6,2},{8,4},{10,6},{12,8},{14,10},{16,12},{18,14},{20,16},{2... | collective-permute-start | bytes 12582920 | tf_op jit(solution)/shard_map/ppermute | solution.py:24
  2379.2 223.4 %collective-permute-start.16 = (bf16[128,8,2048]{2,0,1:T(8,128)(2,1)}, bf16[128,8,2048]{2,0,1:T(8,128)(2,1)}, u32[]{:S(2)}, u32[]{:S(2)}) collective-permute-start(bf16[128,8,2048]{2,0,1:T(8,128)(2,1)} %get-tuple-element.480), channel_id=1, source_target_pairs={{2,0},{4,2},{6,4},{8,6},{10,8},{12,10},{14,12},{16,14},{18,16},{20... | collective-permute-start | bytes 12582920 | tf_op jit(solution)/shard_map/ppermute | solution.py:24
  (92 other events, 8895.7 us)
Sparse Core Ops, SparseCore 0:
  2643.7 516.9 all-reduce.2
where the time goes:
time: 3190 us; the launch traced here: 3170 us
  waiting for transfers between devices  1590 us (50%)
  matrix products  498 us (16%)
  starting transfers between devices  451 us (14%)
  local copies, waits for them, and re-layouts  409 us (13%)
  other arithmetic  191 us (6%)
    ppermute x24, waiting for transfers between devices, passed_along(): return lax.ppermute(x, axis, pairs)  1080 us
    psum x1, waiting for transfers between devices, body(): lax.psum((down_map_gradient, up_map_gradient), ('seq', 'batch'))  510 us
    ppermute x24, starting transfers between devices, passed_along(): return lax.ppermute(x, axis, pairs)  451 us
    dynamic_update_slice x18, local copies, waits for them, and re-layouts, body(): lax.map(visit_keys, jnp.arange(total_rows // block_width, dtype=jnp.int32))  153 us
    dot_general x9, matrix products, query_step(): jnp.einsum('rhqk,rkhe->rqhe', grad_scores, key_heads, preferred_element_t...  104 us
    unnamed x131, local copies, waits for them, and re-layouts  102 us
    slice x27, local copies, waits for them, and re-layouts, block_scores(): value_heads = split_heads(key_block[..., half_width:])  97.3 us
    dot_general x9, matrix products, key_step(): jnp.einsum('rhqk,rqhe->rkhe', grad_scores, query_side[0], preferred_eleme...  87.5 us
  transfers between devices with their start and end apart: 25, of which 13 were waited for; matrix products, arithmetic and copies ran while one was open for 9% of the time, Pallas kernels for 0%

commit v1 on v0

v1 whole, which is shorter than its diff:
```python
import functools

import jax
import jax.numpy as jnp
from jax import lax
from jax.experimental import pallas as pl
from jax.experimental.pallas import tpu as pltpu
from jax.sharding import PartitionSpec as P

HEADS = 16
EXAMPLE_MAX = 1024
SEGMENT_SLOTS = 8
LANES = 128
QUERY_BLOCK = 256

norm_eps = 1e-05
adapter_scale = 8.0
learning_step_size = 3e-05
velocity_factor = 0.5
mean_decay_factor = 0.5
masked_score = -1e30
score_scale = 0.125


def norm_layer(values, gain_row, shift_row):
    average = jnp.mean(values, axis=-1, keepdims=True)
    centred = values - average
    variance = jnp.mean(centred * centred, axis=-1, keepdims=True)
    return centred * lax.rsqrt(variance + norm_eps) * gain_row + shift_row


def matmul_rows(left_side, right_side):
    return lax.dot_general(
        left_side, right_side, (((1,), (0,)), ((), ())), preferred_element_type=jnp.float32
    )


def matmul_back(left_side, right_side):
    return lax.dot_general(
        left_side, right_side, (((1,), (1,)), ((), ())), preferred_element_type=jnp.float32
    )


def matmul_over(left_side, right_side):
    return lax.dot_general(
        left_side, right_side, (((0,), (0,)), ((), ())), preferred_element_type=jnp.float32
    )


def gelu_tanh(values):
    return jax.nn.gelu(values, approximate=True)


def rows_home(x):
    cores = lax.axis_size("batch")
    rows, tokens, width = x.shape
    stripe = tokens // cores
    y = lax.all_to_all(x.reshape(rows, cores, stripe, width), "batch", 1, 0)
    y = y.reshape(cores * rows, stripe, width)
    y = lax.all_to_all(y, "seq", 0, 0, tiled=True)
    return y.reshape(cores * rows * stripe, width)


def rows_back(y, rows, tokens):
    cores = lax.axis_size("batch")
    stripe = tokens // cores
    width = y.shape[-1]
    y = lax.all_to_all(y.reshape(cores * rows, stripe, width), "seq", 0, 0, tiled=True)
    y = lax.all_to_all(y.reshape(cores, rows, stripe, width), "batch", 0, 1)
    return y.reshape(rows, tokens, width)


def row_codes(codes):
    cores = lax.axis_size("batch")
    rows, tokens = codes.shape
    y = jnp.broadcast_to(codes[None], (cores, rows, tokens))
    y = lax.all_to_all(y, "batch", 0, 0, tiled=True).reshape(cores * rows, tokens)
    return lax.all_to_all(y, "seq", 0, 0, tiled=True)


def from_core(x, by):
    cores = lax.axis_size("batch")
    return lax.ppermute(x, "batch", [(i, (i + by) % cores) for i in range(cores)])


def sum_everywhere(x):
    for axis in ("batch", "seq"):
        size = lax.axis_size(axis)
        step = 1
        while step < size:
            x = x + lax.ppermute(x, axis, [(i, i ^ step) for i in range(size)])
            step *= 2
    return x


def lane_masks(dtype):
    lane = lax.broadcasted_iota(jnp.int32, (1, LANES), 1)
    first = (lane < LANES // 2).astype(jnp.float32).astype(dtype)
    second = (lane >= LANES // 2).astype(jnp.float32).astype(dtype)
    return first, second


def block_of(ref, index):
    return ref[pl.ds(index * QUERY_BLOCK, QUERY_BLOCK), :]


def attend_kernel(cores, reach, *refs):
    query_ref, mark_ref = refs[0], refs[1]
    key_refs = refs[2 : 2 + cores]
    value_refs = refs[2 + cores : 2 + 2 * cores]
    key_mark_refs = refs[2 + 2 * cores : 2 + 3 * cores]
    causal_ref = refs[2 + 3 * cores]
    out_ref, log_ref = refs[3 + 3 * cores :]
    masks = lane_masks(jnp.bfloat16)
    lane = lax.broadcasted_iota(jnp.int32, (1, LANES), 1)
    in_first = lane < LANES // 2
    blocks = query_ref.shape[0] // QUERY_BLOCK
    scale = jnp.asarray(score_scale, jnp.bfloat16)
    for n in range(blocks):
        query = block_of(query_ref, n) * scale
        mark = block_of(mark_ref, n)
        results = []
        for own, other in (masks, masks[::-1]):
            query_head = query * own + mark * other
            tiles = []
            for j in range(max(0, n - reach), n + 1):
                for k in range(cores):
                    key_head = block_of(key_refs[k], j) * own + block_of(key_mark_refs[k], j) * other
                    score = matmul_back(query_head, key_head)
                    if j == n:
                        score = score + causal_ref[k]
                    tiles.append((score, k, j))
            top = tiles[0][0]
            for score, _, _ in tiles[1:]:
                top = jnp.maximum(top, score)
            top = jnp.max(top, axis=-1, keepdims=True)
            total = jnp.zeros((QUERY_BLOCK, LANES), jnp.float32)
            for score, k, j in tiles:
                weight = jnp.exp(score - top).astype(jnp.bfloat16)
                value_head = block_of(value_refs[k], j) * own + other
                total = total + matmul_rows(weight, value_head)
            results.append((total, top))
        (first, first_top), (second, second_top) = results
        swapped = jnp.where(in_first, second, first)
        both = jnp.where(in_first, first, second)
        rows = pl.ds(n * QUERY_BLOCK, QUERY_BLOCK)
        out_ref[rows, :] = (both / pltpu.roll(swapped, LANES // 2, 1)).astype(out_ref.dtype)
        log_ref[rows, :] = jnp.log(swapped) + jnp.where(in_first, second_top, first_top)


def spread(wide):
    high = wide.astype(jnp.bfloat16)
    rest = wide - high.astype(jnp.float32)
    middle = rest.astype(jnp.bfloat16)
    low = (rest - middle.astype(jnp.float32)).astype(jnp.bfloat16)
    return high, middle, low


def pull_kernel(cores, reach, *refs):
    query_ref, mark_ref, grad_ref, out_ref, log_ref = refs[:5]
    key_refs = refs[5 : 5 + cores]
    value_refs = refs[5 + cores : 5 + 2 * cores]
    key_mark_refs = refs[5 + 2 * cores : 5 + 3 * cores]
    causal_ref = refs[5 + 3 * cores]
    outs = refs[6 + 3 * cores :]
    grad_query_ref = outs[0]
    grad_key_refs = outs[1 : 1 + cores]
    grad_value_refs = outs[1 + cores : 1 + 2 * cores]
    query_heads, grad_heads, turned = outs[1 + 2 * cores :]
    own_first, own_second = lane_masks(jnp.bfloat16)
    lane = lax.broadcasted_iota(jnp.int32, (1, LANES), 1)
    slot = lax.rem(lane, LANES // 2)
    picks = [
        (slot == SEGMENT_SLOTS + i).astype(jnp.float32).astype(jnp.bfloat16) for i in range(3)
    ]
    value_mark = -(picks[0] + picks[1] + picks[2])
    row = lax.broadcasted_iota(jnp.int32, (LANES, LANES), 0)
    column = lax.broadcasted_iota(jnp.int32, (LANES, LANES), 1)
    across = ((row < LANES // 2) != (column < LANES // 2)).astype(jnp.float32).astype(jnp.bfloat16)
    blocks = query_ref.shape[0] // QUERY_BLOCK
    scale = jnp.asarray(score_scale, jnp.bfloat16)
    heads = ((own_first, own_second), (own_second, own_first))
    for n in range(blocks):
        rows = pl.ds(n * QUERY_BLOCK, QUERY_BLOCK)
        query = query_ref[rows, :] * scale
        grad = grad_ref[rows, :]
        product = grad.astype(jnp.float32) * out_ref[rows, :].astype(jnp.float32)
        high, middle, _ = spread(product)
        dots = matmul_rows(high, across) + matmul_rows(middle, across)
        high, middle, low = spread(dots)
        grad_mark = high * picks[0] + middle * picks[1] + low * picks[2]
        high, middle, low = spread(log_ref[rows, :])
        mark = mark_ref[rows, :] + high * picks[0] + middle * picks[1] + low * picks[2]
        for h, (own, other) in enumerate(heads):
            query_heads[h, rows, :] = query * own + mark * other
            grad_heads[h, rows, :] = grad * own + grad_mark * other
    turned[...] = jnp.zeros_like(turned)
    half = LANES // 2
    for j in range(blocks):
        for k in range(cores):
            key = block_of(key_refs[k], j)
            value = block_of(value_refs[k], j)
            key_mark = block_of(key_mark_refs[k], j)
            grad_key = [None, None]
            grad_value = [None, None]
            for n in range(j, min(blocks, j + reach + 1)):
                rows = pl.ds(n * QUERY_BLOCK, QUERY_BLOCK)
                for h, (own, other) in enumerate(heads):
                    query_head = query_heads[h, rows, :]
                    grad_head = grad_heads[h, rows, :]
                    score = matmul_back(key * own + key_mark * other, query_head)
                    if j == n:
                        score = score + causal_ref[k]
                    weight = jnp.exp(score)
                    change = matmul_back(value * own + value_mark * other, grad_head)
                    change = (weight * change).astype(jnp.bfloat16)
                    weight = weight.astype(jnp.bfloat16)
                    part = matmul_rows(weight, grad_head)
                    grad_value[h] = part if grad_value[h] is None else grad_value[h] + part
                    part = matmul_rows(change, query_head)
                    grad_key[h] = part if grad_key[h] is None else grad_key[h] + part
                    turn = matmul_over(key * own, change)
                    turned[pl.ds(h * half, half), rows] += turn[h * half : (h + 1) * half, :]
            rows = pl.ds(j * QUERY_BLOCK, QUERY_BLOCK)
            in_first = lane < half
            grad_key_refs[k][rows, :] = jnp.where(in_first, *grad_key).astype(jnp.bfloat16)
            grad_value_refs[k][rows, :] = jnp.where(in_first, *grad_value).astype(jnp.bfloat16)
    grad_query_ref[...] = (turned[...].T * score_scale).astype(jnp.bfloat16)


def attention_calls(tokens, width, cores, reach):
    pair = pl.BlockSpec((tokens, LANES), lambda p: (0, p))
    fixed = pl.BlockSpec((tokens, LANES), lambda p: (0, 0))
    causal = pl.BlockSpec((cores, QUERY_BLOCK, QUERY_BLOCK), lambda p: (0, 0, 0))
    grid = (width // LANES,)
    blocks = tokens // QUERY_BLOCK
    pairs = sum(min(n, reach) + 1 for n in range(blocks)) * cores * QUERY_BLOCK**2 * HEADS
    head_width = width // HEADS
    low = jax.ShapeDtypeStruct((tokens, width), jnp.bfloat16)
    wide = jax.ShapeDtypeStruct((tokens, width), jnp.float32)
    params = pltpu.CompilerParams(
        dimension_semantics=("arbitrary",), vmem_limit_bytes=48 * 1024 * 1024
    )
    forward = pl.pallas_call(
        functools.partial(attend_kernel, cores, reach),
        grid=grid,
        in_specs=[pair, fixed] + [pair] * (2 * cores) + [fixed] * cores + [causal],
        out_specs=[pair, pair],
        out_shape=[low, wide],
        compiler_params=params,
        cost_estimate=pl.CostEstimate(
            flops=4 * pairs * head_width,
            bytes_accessed=2 * tokens * width * (4 + 2 * cores),
            transcendentals=pairs,
        ),
        name="attend",
    )
    backward = pl.pallas_call(
        functools.partial(pull_kernel, cores, reach),
        grid=grid,
        in_specs=[pair, fixed, pair, pair, pair]
        + [pair] * (2 * cores)
        + [fixed] * cores
        + [causal],
        out_specs=[pair] * (1 + 2 * cores),
        out_shape=[low] * (1 + 2 * cores),
        scratch_shapes=[
            pltpu.VMEM((2, tokens, LANES), jnp.bfloat16),
            pltpu.VMEM((2, tokens, LANES), jnp.bfloat16),
            pltpu.VMEM((LANES, tokens), jnp.float32),
        ],
        compiler_params=params,
        cost_estimate=pl.CostEstimate(
            flops=10 * pairs * head_width,
            bytes_accessed=2 * tokens * width * (6 + 4 * cores),
            transcendentals=pairs,
        ),
        name="pull",
    )
    return forward, backward


def body(
    inputs,
    segments,
    groups,
    group_loss_weight,
    attention_norm_gain,
    attention_norm_bias,
    query_key_value_weight,
    query_value_bias,
    attention_out_weight,
    attention_out_bias,
    feedforward_norm_gain,
    feedforward_norm_bias,
    expand_weight,
    expand_bias,
    contract_weight,
    contract_bias,
    adapter_down_maps,
    adapter_up_maps,
    down_velocity,
    up_velocity,
    running_down_mean,
    running_up_mean,
    cotangent,
):
    rows_here, tokens_here, width = inputs.shape
    cores = lax.axis_size("batch")
    ring = lax.axis_size("seq")
    assert rows_here * cores == ring
    stripe = tokens_here // cores
    tokens = ring * stripe
    span = QUERY_BLOCK * cores
    reach = -(-(EXAMPLE_MAX - 1) // span)
    rank = adapter_down_maps.shape[-1]
    core = lax.axis_index("batch")
    attend, pull = attention_calls(tokens, width, cores, reach)

    codes = row_codes(segments * SEGMENT_SLOTS + groups).reshape(ring, cores, stripe)
    values_in = rows_home(inputs).astype(jnp.float32)
    cotangent_home = rows_home(cotangent)

    def codes_of(which):
        return lax.dynamic_index_in_dim(codes, which, 1, keepdims=False).reshape(tokens)

    own_codes = codes_of(core)
    own_groups = lax.rem(own_codes, SEGMENT_SLOTS)
    slot = jnp.arange(LANES, dtype=jnp.int32) % (LANES // 2)

    def one_hot(code_row):
        return (code_row // SEGMENT_SLOTS)[:, None] == slot[None, :]

    query_mark = jnp.where(one_hot(own_codes), masked_score, 0.0).astype(jnp.bfloat16)
    place = jnp.arange(QUERY_BLOCK, dtype=jnp.int32)
    place = tokens_here * (place // stripe) + place % stripe
    key_marks, after = [], []
    for by in range(cores):
        which = lax.rem(core - by + cores, cores)
        key_mark = jnp.where(
            slot[None, :] < SEGMENT_SLOTS,
            1.0 - one_hot(codes_of(which)).astype(jnp.float32),
            jnp.where(slot[None, :] < SEGMENT_SLOTS + 3, -1.0, 0.0),
        )
        key_marks.append(key_mark.astype(jnp.bfloat16))
        key_place = place + stripe * which
        after.append(key_place[None, :] > (place + stripe * core)[:, None])
    causal = jnp.where(jnp.stack(after), masked_score, 0.0).astype(jnp.float32)
    causal_turned = jnp.transpose(causal, (0, 2, 1))

    def first_norm(values):
        return norm_layer(
            values, attention_norm_gain.astype(jnp.float32), attention_norm_bias.astype(jnp.float32)
        )

    def second_norm(values):
        return norm_layer(
            values,
            feedforward_norm_gain.astype(jnp.float32),
            feedforward_norm_bias.astype(jnp.float32),
        )

    normed_low = first_norm(values_in).astype(jnp.bfloat16)
    down_reduced = adapter_down_maps.astype(jnp.bfloat16)
    up_reduced = adapter_up_maps.astype(jnp.bfloat16)
    bias_as_float = query_value_bias.astype(jnp.float32)

    def projected(which):
        return matmul_rows(normed_low, query_key_value_weight[:, which * width : (which + 1) * width])

    lora_down = [matmul_rows(normed_low, down_reduced[j]).astype(jnp.bfloat16) for j in range(2)]
    lora_up = [adapter_scale * matmul_rows(lora_down[j], up_reduced[j]) for j in range(2)]
    keys = projected(1).astype(jnp.bfloat16)
    values = (projected(2) + bias_as_float[1] + lora_up[1]).astype(jnp.bfloat16)
    queries = (projected(0) + bias_as_float[0] + lora_up[0]).astype(jnp.bfloat16)
    all_keys = [keys] + [from_core(keys, by) for by in range(1, cores)]
    all_values = [values] + [from_core(values, by) for by in range(1, cores)]
    attended, log_total = attend(queries, query_mark, *all_keys, *all_values, *key_marks, causal)
    middle = (
        values_in
        + matmul_rows(attended, attention_out_weight)
        + attention_out_bias.astype(jnp.float32)
    )
    normed_two = second_norm(middle).astype(jnp.bfloat16)
    pre_act = matmul_rows(normed_two, expand_weight) + expand_bias.astype(jnp.float32)
    act_low = gelu_tanh(pre_act).astype(jnp.bfloat16)
    layer_result = middle + matmul_rows(act_low, contract_weight) + contract_bias.astype(jnp.float32)
    layer_out = rows_back(layer_result.astype(jnp.bfloat16), rows_here, tokens_here)

    chooser = own_groups[:, None] == jnp.arange(group_loss_weight.shape[0], dtype=jnp.int32)
    token_weight = jnp.sum(jnp.where(chooser, group_loss_weight[None, :], 0.0), axis=-1)
    grad_out = cotangent_home.astype(jnp.float32) * token_weight[:, None]
    grad_act = matmul_back(grad_out.astype(jnp.bfloat16), contract_weight)
    _, gelu_pull = jax.vjp(gelu_tanh, pre_act)
    grad_pre = gelu_pull(grad_act)[0].astype(jnp.bfloat16)
    _, second_pull = jax.vjp(second_norm, middle)
    grad_middle = grad_out + second_pull(matmul_back(grad_pre, expand_weight))[0]
    grad_attended = matmul_back(grad_middle.astype(jnp.bfloat16), attention_out_weight).astype(
        jnp.bfloat16
    )
    pulled = pull(
        queries,
        query_mark,
        grad_attended,
        attended,
        log_total,
        *all_keys,
        *all_values,
        *key_marks,
        causal_turned,
    )
    grad_queries = pulled[0]

    def owned(parts):
        total = parts[0].astype(jnp.float32)
        for by in range(1, cores):
            total = total + from_core(parts[by], -by).astype(jnp.float32)
        return total.astype(jnp.bfloat16)

    grad_keys = owned(pulled[1 : 1 + cores])
    grad_values = owned(pulled[1 + cores :])
    incoming = (grad_queries, grad_values)
    up_parts = [adapter_scale * matmul_over(lora_down[j], incoming[j]) for j in range(2)]
    grad_down = [
        (adapter_scale * matmul_back(incoming[j], up_reduced[j])).astype(jnp.bfloat16)
        for j in range(2)
    ]
    down_parts = [matmul_over(grad_down[j], normed_low) for j in range(2)]
    adapter_sums = sum_everywhere(jnp.concatenate(up_parts + down_parts, axis=0))
    adapter_sums = adapter_sums.reshape(2, 2, rank, width)
    up_map_gradient = adapter_sums[0]
    down_map_gradient = jnp.transpose(adapter_sums[1], (0, 2, 1))
    grad_normed = matmul_back(
        jnp.concatenate([grad_queries, grad_keys, grad_values], axis=-1), query_key_value_weight
    )
    for j in range(2):
        grad_normed = grad_normed + matmul_back(grad_down[j], down_reduced[j])
    _, first_pull = jax.vjp(first_norm, values_in)
    input_grad = (grad_middle + first_pull(grad_normed)[0]).astype(jnp.bfloat16)
    input_grad = rows_back(input_grad, rows_here, tokens_here)

    down_velocity_next = velocity_factor * down_velocity + down_map_gradient
    up_velocity_next = velocity_factor * up_velocity + up_map_gradient
    adapter_down_updated = adapter_down_maps - learning_step_size * (
        down_map_gradient + velocity_factor * down_velocity_next
    )
    adapter_up_updated = adapter_up_maps - learning_step_size * (
        up_map_gradient + velocity_factor * up_velocity_next
    )
    updated_down_mean = (
        mean_decay_factor * running_down_mean + (1.0 - mean_decay_factor) * adapter_down_updated
    )
    updated_up_mean = (
        mean_decay_factor * running_up_mean + (1.0 - mean_decay_factor) * adapter_up_updated
    )
    return (
        layer_out,
        input_grad,
        down_map_gradient,
        up_map_gradient,
        adapter_down_updated,
        adapter_up_updated,
        down_velocity_next,
        up_velocity_next,
        updated_down_mean,
        updated_up_mean,
        adapter_down_updated.astype(jnp.bfloat16),
        adapter_up_updated.astype(jnp.bfloat16),
    )


def solution(mesh):
    tokens = P("batch", "seq", None)
    codes = P("batch", "seq")
    return jax.shard_map(
        body,
        mesh=mesh,
        in_specs=(tokens, codes, codes) + (P(),) * 19 + (tokens,),
        out_specs=(tokens, tokens) + (P(),) * 10,
        check_vma=False,
    )
```

time: 3190 us -> 468 us (0.15)
  waiting for transfers between devices: 1590 us -> 80.8 us
  starting transfers between devices: 451 us -> 44.3 us
  local copies, waits for them, and re-layouts: 409 us -> 15.7 us
  matrix products: 498 us -> 121 us
  other arithmetic: 191 us -> 36.4 us
  Pallas kernels: 0 us -> 118 us
  blocking collectives: 0 us -> 46 us
    ppermute x24 -> x9, waiting for transfers between devices: 1080 us -> 38 us  [the longest x5 38 us: sum_everywhere(): x = x + lax.ppermute(x, axis, [(i, i ^ step) for i in range(size)])]
    psum x1 -> x0, waiting for transfers between devices: 510 us -> none  [body(): lax.psum((down_map_gradient, up_map_gradient), ('seq', 'batch'))]
    ppermute x24 -> x9, starting transfers between devices: 451 us -> 9.21 us  [the longest x5 8.14 us: sum_everywhere(): x = x + lax.ppermute(x, axis, [(i, i ^ step) for i in range(size)])]
    dot_general x77 -> x21, matrix products: 498 us -> 121 us  [the longest x7 60.5 us: matmul_back(): lax.dot_general(left_side, right_side, (((1,), (1,)), ((), ())), preferre...]
    dynamic_update_slice x18 -> x0, local copies, waits for them, and re-layouts: 153 us -> none  [body(): lax.map(visit_keys, jnp.arange(total_rows // block_width, dtype=jnp.int32))]
    pallas_call x0 -> x2, Pallas kernels: none -> 118 us  [the longest x1 78.3 us: body(): pull(queries, query_mark, grad_attended, attended, log_total, *all_keys,...]
    unnamed x131 -> x126, local copies, waits for them, and re-layouts: 102 us -> 3.4 us
    slice x29 -> x2, local copies, waits for them, and re-layouts: 97.7 us -> 0.02 us  [the longest x1 0.01 us: body(): values = (projected(2) + bias_as_float[1] + lora_up[1]).astype(jnp.bfloat16)]
  transfers between devices with their start and end apart: 25 -> 14, of which waited for: 13 -> 7; matrix products, arithmetic and copies ran while one was open for 9% -> 27% of each run, Pallas kernels for 0% -> 9%
where the time goes in v1:
time: 468 us; the launch traced here: 464 us
  matrix products  121 us (26%)
  Pallas kernels  118 us (25%)
  waiting for transfers between devices  80.8 us (17%)
  blocking collectives  46 us (10%)
  starting transfers between devices  44.3 us (9%)
  other arithmetic  36.4 us (8%)
  local copies, waits for them, and re-layouts  15.7 us (3%)
    pallas_call x1, Pallas kernels, body(): pull(queries, query_mark, grad_attended, attended, log_total, *all_keys,...  78.3 us
    dot_general x7, matrix products, matmul_back(): lax.dot_general(left_side, right_side, (((1,), (1,)), ((), ())), preferre...  60.5 us
    dot_general x10, matrix products, matmul_rows(): lax.dot_general(left_side, right_side, (((1,), (0,)), ((), ())), preferre...  55.7 us
    pallas_call x1, Pallas kernels, body(): attend(queries, query_mark, *all_keys, *all_values, *key_marks, causal)  39.4 us
    ppermute x5, waiting for transfers between devices, sum_everywhere(): x = x + lax.ppermute(x, axis, [(i, i ^ step) for i in range(size)])  38 us
    all_to_all x2, waiting for transfers between devices, rows_home(): y = lax.all_to_all(y, 'seq', 0, 0, tiled=True)  38 us
    all_to_all x2, starting transfers between devices, rows_back(): lax.all_to_all(y.reshape(cores * rows, stripe, width), 'seq', 0, 0, tiled...  17.5 us
    all_to_all x1, blocking collectives, row_codes(): return lax.all_to_all(y, 'seq', 0, 0, tiled=True)  15.5 us
  transfers between devices with their start and end apart: 14, of which 7 were waited for; matrix products, arithmetic and copies ran while one was open for 27% of the time, Pallas kernels for 9%

profile of v1, /device:TPU:0, one launch (start us, length us, event | category | flops | bytes accessed | tf_op | source)
XLA Modules:
  0.0 463.9 jit_solution(13122411036079764686)
XLA Ops:
  10.2 8.7 %all_to_all.94 = bf16[1,8,2,64,1024]{4,3,1,0,2:T(8,128)(2,1)} all-to-all(bf16[1,8,2,64,1024]{4,3,1,0,2:T(8,128)(2,1)} %copy.46), channel_id=1, replica_groups=mesh['seq'=16,'batch'=2] {'batch'}, dimensions={2} | all-to-all | bytes 4194304 | tf_op jit(solution)/shard_map/all_to_all | solution.py:58
  18.9 6.5 %all_to_all.95 = bf16[1,8,2,64,1024]{4,3,1,0,2:T(8,128)(2,1)} all-to-all(bf16[1,8,2,64,1024]{4,3,1,0,2:T(8,128)(2,1)S(1)} %copy-done.20), channel_id=1, replica_groups=mesh['seq'=16,'batch'=2] {'batch'}, dimensions={2} | all-to-all | bytes 4194304 | tf_op jit(solution)/shard_map/all_to_all | solution.py:58
  25.4 15.5 %all_to_all.96 = s32[16,1,128]{2,1,0:T(1,128)S(1)} all-to-all(s32[16,1,128]{2,1,0:T(1,128)S(1)} %bitcast.116), channel_id=1, replica_groups=mesh['seq'=16,'batch'=2] {'seq'}, dimensions={0} | all-to-all | bytes 16384 | tf_op jit(solution)/shard_map/all_to_all | solution.py:78
  40.9 4.4 all-to-all-start.1
  50.0 38.0 %all-to-all-done.1 = bf16[16,64,1024]{2,1,0:T(8,128)(2,1)} async-done(((bf16[16,64,1024]{2,1,0:T(8,128)(2,1)}), bf16[16,64,1024]{2,1,0:T(8,128)(2,1)}, u32[]{:S(2)}, u32[]{:S(2)}) %all-to-all-start.1) | async-done | bytes 2097184 | tf_op jit(solution)/shard_map/all_to_all | solution.py:60
  88.0 9.9 %all-to-all-start.7 = ((bf16[16,64,1024]{2,1,0:T(8,128)(2,1)}), bf16[16,64,1024]{2,1,0:T(8,128)(2,1)}, u32[]{:S(2)}, u32[]{:S(2)}) async-start(bf16[16,64,1024]{2,1,0:T(8,128)(2,1)} %bitcast.107), calls=%async_computation.7 | async-start | bytes 4194304 | tf_op jit(solution)/shard_map/all_to_all | solution.py:60
  104.7 6.0 %fusion.58.refs_2_.refs_5_ = bf16[1024,1024]{1,0:T(8,128)(2,1)} fusion(bf16[1024,1024]{1,0:T(8,128)(2,1)S(1)} %fusion.29, bf16[1024,3072]{1,0:T(8,128)(2,1)} %param.29), kind=kOutput, calls=%fused_computation.68 | convolution fusion | flops 2148532224 | bytes 6291456 | tf_op jit(solution)/shard_map/dot_general | solution.py:33
  123.7 4.6 fusion.54
  129.1 39.4 %attend.1 = (bf16[1024,1024]{1,0:T(8,128)(2,1)S(1)}, f32[1024,1024]{1,0:T(8,128)}) custom-call(bf16[1024,1024]{1,0:T(8,128)(2,1)S(1)} %add_convert_fusion.6.refs_0_, bf16[1024,128]{1,0:T(8,128)(2,1)S(1)} %select_convert_fusion.2.refs_1_, bf16[1024,1024]{1,0:T(8,128)(2,1)} %fusion.58.refs_2_.refs_5_, bf16[1024,1024]{1,0:T(8,128)(2,1)} %collective-permute-done.refs_3_.refs_6_, ...), custom_call_target="tpu_custom_call" | custom-call | flops 4831838208 | bytes 16777216 | tf_op jit(solution)/shard_map/attend/pallas_call | solution.py:378
  168.6 4.8 %fusion.98 = (f32[1024]{0:T(1024)S(1)}, f32[1024,1024]{1,0:T(8,128)S(1)}) fusion(f32[1024]{0:T(1024)S(1)} %convert_element_type.164, bf16[1024,1024]{1,0:T(8,128)(2,1)S(1)} %get-tuple-element.19.refs_3_, bf16[1024,1024]{1,0:T(8,128)(2,1)S(1)} %copy-done, bf16[16,64,1024]{2,1,0:T(8,128)(2,1)} %all-to-all-done.1), kind=kOutput, calls=%fused_computation.167 | convolution fusion | flops 2151676928 | bytes 10493952 | tf_op jit(solution)/shard_map/dot_general | solution.py:33
  175.5 12.6 %fusion.35 = f32[1024,4096]{1,0:T(8,128)} fusion(bf16[1024,4096]{1,0:T(8,128)(2,1)S(1)} %bitcast.120, f32[1024,1024]{1,0:T(8,128)S(1)} %get-tuple-element.52, f32[1024]{0:T(1024)S(1)} %convert_element_type.166, f32[1024]{0:T(1024)S(1)} %convert_element_type.165, f32[1024]{0:T(1024)S(1)} %fusion.74, f32[1024]{0:T(1024)S(1)} %broadcast_multiply_fusion.1), kind=kOutput, calls=%fused_computation.53 | convolution fusion | flops 8595177472 | bytes 29376512 | tf_op jit(solution)/shard_map/dot_general | solution.py:33
  188.0 31.8 %multiply_reduce_fusion = (f32[1024]{0:T(1024)S(1)}, f32[1024,1024]{1,0:T(8,128)}) fusion(f32[1024,1024]{1,0:T(8,128)} %copy-done.16, f32[1024]{0:T(1024)S(1)} %convert_element_type.165, f32[1024]{0:T(1024)S(1)} %broadcast_multiply_fusion.1, bf16[1024,4096]{1,0:T(8,128)(2,1)} %param.35, f32[1024,4096]{1,0:T(8,128)} %fusion.35, ...), kind=kOutput, calls=%fused_computation.45 | convolution fusion | flops 17275289600 | bytes 44072960 | tf_op jit(solution)/shard_map/dot_general | solution.py:39
  224.2 6.8 %fusion.61.refs_2_ = bf16[1024,1024]{1,0:T(8,128)(2,1)} fusion(bf16[1024,1024]{1,0:T(8,128)(2,1)S(1)} %copy-done, f32[1024,1024]{1,0:T(8,128)S(1)} %get-tuple-element.36, bf16[1024,1024]{1,0:T(8,128)(2,1)} %bitcast.36, f32[1024]{0:T(1024)S(1)} %negate_multiply_fusion.1, f32[1024]{0:T(1024)S(1)} %select_reduce_fusion), kind=kOutput, calls=%fused_computation.69 | convolution fusion | flops 2153775104 | bytes 10493952 | tf_op jit(solution)/shard_map/dot_general | solution.py:39
  231.0 78.3 %pull.1 = (bf16[1024,1024]{1,0:T(8,128)(2,1)S(1)}, bf16[1024,1024]{1,0:T(8,128)(2,1)S(1)}, bf16[1024,1024]{1,0:T(8,128)(2,1)}, bf16[1024,1024]{1,0:T(8,128)(2,1)}, bf16[1024,1024]{1,0:T(8,128)(2,1)}) custom-call(bf16[1024,1024]{1,0:T(8,128)(2,1)} %copy-done.5, bf16[1024,128]{1,0:T(8,128)(2,1)S(1)} %copy-done.9, bf16[1024,1024]{1,0:T(8,128)(2,1)} %fusion.61.refs_2_, ...), custom_call_target="tpu_custom_call" | custom-call | flops 12079595520 | bytes 29360128 | tf_op jit(solution)/shard_map/pull/pallas_call | solution.py:401
  311.1 17.9 %add_convert_fusion.3 = bf16[1024,1024]{1,0:T(8,128)(2,1)} fusion(f32[1024,1024]{1,0:T(8,128)S(1)} %copy-done.17, f32[1024]{0:T(1024)S(1)} %copy-done.53, bf16[4096,1024]{1,0:T(8,128)(2,1)} %param.37, f32[1024,4096]{1,0:T(8,128)} %fusion.35, f32[4096]{0:T(1024)S(1)} %convert_element_type.168), kind=kOutput, calls=%fused_computation.46 | convolution fusion | flops 8635023360 | bytes 31477760 | tf_op jit(solution)/shard_map/dot_general | solution.py:33
  329.1 7.4 %all-to-all-start.4 = ((bf16[16,64,1024]{2,1,0:T(8,128)(2,1)}), bf16[16,64,1024]{2,1,0:T(8,128)(2,1)}, u32[]{:S(2)}, u32[]{:S(2)}) async-start(bf16[16,64,1024]{2,1,0:T(8,128)(2,1)} %bitcast.112), calls=%async_computation.4 | async-start | bytes 4194304 | tf_op jit(solution)/shard_map/all_to_all | solution.py:68
  352.0 13.3 %fusion.30 = (f32[1024]{0:T(1024)S(1)}, f32[1024,1024]{1,0:T(8,128)}) fusion(bf16[16,64,1024]{2,1,0:T(8,128)(2,1)} %all-to-all-done.1, f32[1024]{0:T(1024)S(1)} %copy-done.40, f32[1024]{0:T(1024)S(1)} %copy-done.46, f32[1024,1024]{1,0:T(8,128)} %fusion.68, f32[1024,1024]{1,0:T(8,128)} %fusion.67, bf16[1024,3072]{1,0:T(8,128)(2,1)} %param.29, ...), kind=kOutput, calls=%fused_computation.39 | convolution fusion | flops 6468664320 | bytes 27275264 | tf_op jit(solution)/shard_map/dot_general | solution.py:39
  369.4 5.5 %add_convert_fusion = bf16[1024,1024]{1,0:T(8,128)(2,1)} fusion(f32[1024,1024]{1,0:T(8,128)S(1)} %copy-done.19, bf16[16,64,1024]{2,1,0:T(8,128)(2,1)} %all-to-all-done.7, f32[1024]{0:T(1024)S(1)} %negate_multiply_fusion, f32[1024]{0:T(1024)S(1)} %negate_multiply_fusion.1, f32[1024]{0:T(1024)S(1)} %select_reduce_fusion, f32[1024]{0:T(1024)S(1)} %multiply_multiply_fusion.2, ...), kind=kLoop, calls=%fused_computation.41 | loop fusion | flops 13631488 | bytes 14704640 | tf_op jit(solution)/shard_map/convert_element_type | solution.py:439
  374.9 4.8 %all-to-all-done.4 = bf16[16,64,1024]{2,1,0:T(8,128)(2,1)} async-done(((bf16[16,64,1024]{2,1,0:T(8,128)(2,1)}), bf16[16,64,1024]{2,1,0:T(8,128)(2,1)}, u32[]{:S(2)}, u32[]{:S(2)}) %all-to-all-start.4) | async-done | bytes 2097184 | tf_op jit(solution)/shard_map/all_to_all | solution.py:68
  379.7 8.7 %all_to_all.97 = bf16[2,8,1,64,1024]{4,3,1,2,0:T(8,128)(2,1)} all-to-all(bf16[2,8,1,64,1024]{4,3,1,2,0:T(8,128)(2,1)} %bitcast.14), channel_id=1, replica_groups=mesh['seq'=16,'batch'=2] {'batch'}, dimensions={0} | all-to-all | bytes 4194304 | tf_op jit(solution)/shard_map/all_to_all | solution.py:69
  388.4 10.1 %all-to-all-start.8 = ((bf16[16,64,1024]{2,1,0:T(8,128)(2,1)}), bf16[16,64,1024]{2,1,0:T(8,128)(2,1)}, u32[]{:S(2)}, u32[]{:S(2)}) async-start(bf16[16,64,1024]{2,1,0:T(8,128)(2,1)} %bitcast.109), calls=%async_computation.8 | async-start | bytes 4194304 | tf_op jit(solution)/shard_map/all_to_all | solution.py:68
  415.5 19.1 %collective-permute-done.7 = f32[16,1024]{1,0:T(8,128)S(1)} collective-permute-done((f32[16,1024]{1,0:T(8,128)S(1)}, f32[16,1024]{1,0:T(8,128)S(1)}, u32[]{:S(2)}, u32[]{:S(2)}) %collective-permute-start.7) | collective-permute-done | bytes 65568 | tf_op jit(solution)/shard_map/ppermute | solution.py:91
  438.7 11.0 %collective-permute-done.8 = f32[16,1024]{1,0:T(8,128)S(1)} collective-permute-done((f32[16,1024]{1,0:T(8,128)S(1)}, f32[16,1024]{1,0:T(8,128)S(1)}, u32[]{:S(2)}, u32[]{:S(2)}) %collective-permute-start.8) | collective-permute-done | bytes 65568 | tf_op jit(solution)/shard_map/ppermute | solution.py:91
  455.6 6.6 %all_to_all.98 = bf16[2,8,1,64,1024]{4,3,1,2,0:T(8,128)(2,1)S(1)} all-to-all(bf16[2,8,1,64,1024]{4,3,1,2,0:T(8,128)(2,1)} %bitcast.25), channel_id=1, replica_groups=mesh['seq'=16,'batch'=2] {'batch'}, dimensions={0} | all-to-all | bytes 4194304 | tf_op jit(solution)/shard_map/all_to_all | solution.py:69
  (229 shorter events, 90.1 us)
Async XLA Ops:
  0.6 168.0 %copy-start = (bf16[1024,1024]{1,0:T(8,128)(2,1)S(1)}, bf16[1024,1024]{1,0:T(8,128)(2,1)}, u32[]{:S(2)}) copy-start(bf16[1024,1024]{1,0:T(8,128)(2,1)} %param.31) | copy-start | bytes 6291460
  2.1 8.0 %all-to-all-start.2 = ((s32[2,8,128]{2,1,0:T(8,128)}), s32[2,8,128]{2,1,0:T(8,128)S(1)}, u32[]{:S(2)}, u32[]{:S(2)}) async-start(s32[2,8,128]{2,1,0:T(8,128)} %broadcast_in_dim.74), calls=%async_computation.2 | async-start | bytes 16384 | tf_op jit(solution)/shard_map/all_to_all | solution.py:77
  40.9 47.0 %all-to-all-start.1 = ((bf16[16,64,1024]{2,1,0:T(8,128)(2,1)}), bf16[16,64,1024]{2,1,0:T(8,128)(2,1)}, u32[]{:S(2)}, u32[]{:S(2)}) async-start(bf16[16,64,1024]{2,1,0:T(8,128)(2,1)} %bitcast.108), calls=%async_computation.1 | async-start | bytes 4194304 | tf_op jit(solution)/shard_map/all_to_all | solution.py:60
  45.4 69.4 %copy-start.45 = (f32[1024]{0:T(1024)}, f32[1024]{0:T(1024)S(1)}, u32[]{:S(2)}) copy-start(f32[1024]{0:T(1024)S(1)} %convert_element_type.146) | copy-start | bytes 12292
  46.1 75.2 %copy-start.23 = (bf16[2,1024,4]{1,2,0:T(4,128)(2,1)}, bf16[2,1024,4]{1,2,0:T(4,128)(2,1)S(1)}, u32[]{:S(2)}) copy-start(bf16[2,1024,4]{1,2,0:T(4,128)(2,1)S(1)} %convert_element_type.152) | copy-start | bytes 49156
  46.2 82.1 %copy-start.25 = (bf16[2,4,1024]{2,1,0:T(4,128)(2,1)}, bf16[2,4,1024]{2,1,0:T(4,128)(2,1)S(1)}, u32[]{:S(2)}) copy-start(bf16[2,4,1024]{2,1,0:T(4,128)(2,1)S(1)} %convert_element_type.154) | copy-start | bytes 49156
  88.0 100.1 %all-to-all-start.7 = ((bf16[16,64,1024]{2,1,0:T(8,128)(2,1)}), bf16[16,64,1024]{2,1,0:T(8,128)(2,1)}, u32[]{:S(2)}, u32[]{:S(2)}) async-start(bf16[16,64,1024]{2,1,0:T(8,128)(2,1)} %bitcast.107), calls=%async_computation.7 | async-start | bytes 4194304 | tf_op jit(solution)/shard_map/all_to_all | solution.py:60
  114.7 14.4 %collective-permute-start = (bf16[1024,1024]{1,0:T(8,128)(2,1)}, bf16[1024,1024]{1,0:T(8,128)(2,1)}, u32[]{:S(2)}, u32[]{:S(2)}) collective-permute-start(bf16[1024,1024]{1,0:T(8,128)(2,1)} %fusion.58.refs_2_.refs_5_), channel_id=1, source_target_pairs={{0,1},{1,0},{2,3},{3,2},{4,5},{5,4},{6,7},{7,6},{8,9},{9,8},{10,11... | collective-permute-start | bytes 6291464 | tf_op jit(solution)/shard_map/ppermute | solution.py:83
  120.0 9.1 %collective-permute-start.1 = (bf16[1024,1024]{1,0:T(8,128)(2,1)}, bf16[1024,1024]{1,0:T(8,128)(2,1)}, u32[]{:S(2)}, u32[]{:S(2)}) collective-permute-start(bf16[1024,1024]{1,0:T(8,128)(2,1)} %add_convert_fusion.5.refs_4_.refs_7_), channel_id=1, source_target_pairs={{0,1},{1,0},{2,3},{3,2},{4,5},{5,4},{6,7},{7,6},{8,9},{9,8},{10,11... | collective-permute-start | bytes 6291464 | tf_op jit(solution)/shard_map/ppermute | solution.py:83
  231.0 80.1 %copy-start.17 = (f32[1024,1024]{1,0:T(8,128)S(1)}, f32[1024,1024]{1,0:T(8,128)}, u32[]{:S(2)}) copy-start(f32[1024,1024]{1,0:T(8,128)} %copy-done.16) | copy-start | bytes 12582916
  231.0 80.1 %copy-start.53 = (f32[1024]{0:T(1024)S(1)}, f32[1024]{0:T(1024)}, u32[]{:S(2)}) copy-start(f32[1024]{0:T(1024)} %convert_element_type.170) | copy-start | bytes 12292
  310.6 34.4 %collective-permute-start.2 = (bf16[1024,1024]{1,0:T(8,128)(2,1)}, bf16[1024,1024]{1,0:T(8,128)(2,1)}, u32[]{:S(2)}, u32[]{:S(2)}) collective-permute-start(bf16[1024,1024]{1,0:T(8,128)(2,1)} %get-tuple-element.23), channel_id=1, source_target_pairs={{0,1},{1,0},{2,3},{3,2},{4,5},{5,4},{6,7},{7,6},{8,9},{9,8},{10,11... | collective-permute-start | bytes 6291464 | tf_op jit(solution)/shard_map/ppermute | solution.py:83
  310.7 31.0 %collective-permute-start.3 = (bf16[1024,1024]{1,0:T(8,128)(2,1)}, bf16[1024,1024]{1,0:T(8,128)(2,1)}, u32[]{:S(2)}, u32[]{:S(2)}) collective-permute-start(bf16[1024,1024]{1,0:T(8,128)(2,1)} %get-tuple-element.25), channel_id=1, source_target_pairs={{0,1},{1,0},{2,3},{3,2},{4,5},{5,4},{6,7},{7,6},{8,9},{9,8},{10,11... | collective-permute-start | bytes 6291464 | tf_op jit(solution)/shard_map/ppermute | solution.py:83
  329.1 50.7 %all-to-all-start.4 = ((bf16[16,64,1024]{2,1,0:T(8,128)(2,1)}), bf16[16,64,1024]{2,1,0:T(8,128)(2,1)}, u32[]{:S(2)}, u32[]{:S(2)}) async-start(bf16[16,64,1024]{2,1,0:T(8,128)(2,1)} %bitcast.112), calls=%async_computation.4 | async-start | bytes 4194304 | tf_op jit(solution)/shard_map/all_to_all | solution.py:68
  388.4 67.1 %all-to-all-start.8 = ((bf16[16,64,1024]{2,1,0:T(8,128)(2,1)}), bf16[16,64,1024]{2,1,0:T(8,128)(2,1)}, u32[]{:S(2)}, u32[]{:S(2)}) async-start(bf16[16,64,1024]{2,1,0:T(8,128)(2,1)} %bitcast.109), calls=%async_computation.8 | async-start | bytes 4194304 | tf_op jit(solution)/shard_map/all_to_all | solution.py:68
  400.7 49.8 %copy-start.47 = (f32[2,1024,4]{1,2,0:T(4,128)S(1)}, f32[2,1024,4]{1,2,0:T(4,128)}, u32[]{:S(2)}) copy-start(f32[2,1024,4]{1,2,0:T(4,128)} %param.43) | copy-start | bytes 98308
  400.7 50.5 %copy-start.32 = (f32[2,4,1024]{2,1,0:T(4,128)S(1)}, f32[2,4,1024]{2,1,0:T(4,128)}, u32[]{:S(2)}) copy-start(f32[2,4,1024]{2,1,0:T(4,128)} %param.40) | copy-start | bytes 98308
  400.7 50.4 %copy-start.50 = (f32[2,4,1024]{2,1,0:T(4,128)S(1)}, f32[2,4,1024]{2,1,0:T(4,128)}, u32[]{:S(2)}) copy-start(f32[2,4,1024]{2,1,0:T(4,128)} %param.42) | copy-start | bytes 98308
  400.7 51.1 %copy-start.48 = (f32[2,4,1024]{2,1,0:T(4,128)S(1)}, f32[2,4,1024]{2,1,0:T(4,128)}, u32[]{:S(2)}) copy-start(f32[2,4,1024]{2,1,0:T(4,128)} %param.44) | copy-start | bytes 98308
  403.6 1.3 collective-permute-start.4
  404.9 4.4 collective-permute-start.5
  409.3 6.1 %collective-permute-start.6 = (f32[16,1024]{1,0:T(8,128)S(1)}, f32[16,1024]{1,0:T(8,128)S(1)}, u32[]{:S(2)}, u32[]{:S(2)}) collective-permute-start(f32[16,1024]{1,0:T(8,128)S(1)} %add.360), channel_id=1, source_target_pairs={{0,4},{2,6},{4,0},{6,2},{8,12},{10,14},{12,8},{14,10},{16,20},{18,... | collective-permute-start | bytes 196616 | tf_op jit(solution)/shard_map/ppermute | solution.py:91
  415.4 19.3 %collective-permute-start.7 = (f32[16,1024]{1,0:T(8,128)S(1)}, f32[16,1024]{1,0:T(8,128)S(1)}, u32[]{:S(2)}, u32[]{:S(2)}) collective-permute-start(f32[16,1024]{1,0:T(8,128)S(1)} %add.361), channel_id=1, source_target_pairs={{0,8},{2,10},{4,12},{6,14},{8,0},{10,2},{12,4},{14,6},{16,24},{18,... | collective-permute-start | bytes 196616 | tf_op jit(solution)/shard_map/ppermute | solution.py:91
  434.7 15.1 %collective-permute-start.8 = (f32[16,1024]{1,0:T(8,128)S(1)}, f32[16,1024]{1,0:T(8,128)S(1)}, u32[]{:S(2)}, u32[]{:S(2)}) collective-permute-start(f32[16,1024]{1,0:T(8,128)S(1)} %add.362), channel_id=1, source_target_pairs={{0,16},{2,18},{4,20},{6,22},{8,24},{10,26},{12,28},{14,30},{16,0},... | collective-permute-start | bytes 196616 | tf_op jit(solution)/shard_map/ppermute | solution.py:91
  (53 other events, 702.6 us)
